TPU v7x, 32 devices: a whole 2x2x4 slice. The times are simulated.
32 devices in a mesh: vol: 16 (over z, x, core), slab: 2 (over y).
Axes of the slice: x: 2, y: 2, z: 4, core: 2. Of those that a mesh axis runs over, the one named last changes fastest.
Arguments:
- volumes: bfloat16 [32, 4, 16, 16, 64], P('vol', None, 'slab'), may hold values from -6 to 6
- w_first: bfloat16 [32, 108], replicated, may hold values from -0.625 to 0.625
- w_second: bfloat16 [64, 864], replicated, may hold values from -0.21875 to 0.21875
- w_third: bfloat16 [128, 1728], replicated, may hold values from -0.15625 to 0.15625
- map_grad: bfloat16 [32, 128, 4, 4, 16], P(('vol', 'slab')), may hold values from -6 to 6
Outputs:
- grad_first: float32 [32, 108], replicated
- grad_second: float32 [64, 864], replicated
- grad_third: float32 [128, 1728], replicated
All inputs are finite; a program needn't handle non-finite values.
Results may differ from a plain program's by a relative error of at most 0.0071.
Values may be sent and summed in bfloat16 or wider, within the bound.
A program may use at most 64 MiB of HBM per device.

v0:
```python
import jax
import jax.numpy as jnp
from jax import lax
from jax.sharding import PartitionSpec as P

FORWARD_DIMS = ("NCDHW", "OIDHW", "NCDHW")
FILTER_DIMS = ("CNDHW", "IODHW", "CNDHW")
SPREAD_DIMS = ("NCDHW", "IODHW", "NCDHW")


def shifted(array, axis, by):
    length = lax.axis_size(axis)
    pairs = [(i, i + by) for i in range(length) if 0 <= i + by < length]
    return lax.ppermute(array, axis, pairs)


def kernel_of(weight):
    channels = weight.shape[1] // 27
    return weight.reshape(weight.shape[0], 3, 3, 3, channels).transpose(0, 4, 1, 2, 3)


def flat_of(kernel):
    return kernel.transpose(0, 2, 3, 4, 1).reshape(kernel.shape[0], -1)


def forward(maps, weight, stride, pads):
    return lax.conv_general_dilated(
        maps,
        kernel_of(weight),
        (stride, stride, stride),
        pads,
        dimension_numbers=FORWARD_DIMS,
        preferred_element_type=jnp.float32,
    )


def weight_grad(maps, delta, stride, pads):
    bounds = []
    for dim_index in range(3):
        extent = maps.shape[2 + dim_index]
        lower = pads[dim_index][0]
        cells_out = delta.shape[2 + dim_index]
        bounds.append((lower, 3 - extent - lower + (cells_out - 1) * stride))
    kernel = lax.conv_general_dilated(
        maps,
        delta,
        (1, 1, 1),
        bounds,
        rhs_dilation=(stride, stride, stride),
        dimension_numbers=FILTER_DIMS,
        preferred_element_type=jnp.float32,
    )
    return flat_of(kernel)


def spread_back(delta, weight, stride):
    kernel = kernel_of(weight)[:, :, ::-1, ::-1, ::-1]
    return lax.conv_general_dilated(
        delta,
        kernel,
        (1, 1, 1),
        ((2, 2), (2, 2), (2, 2)),
        lhs_dilation=(stride, stride, stride),
        dimension_numbers=SPREAD_DIMS,
        preferred_element_type=jnp.float32,
    )


def interior(full, shape):
    return full[:, :, 1 : 1 + shape[2], 1 : 1 + shape[3], 1 : 1 + shape[4]]


def silu_slope(pre):
    sigma = jax.nn.sigmoid(pre)
    return sigma * (1.0 + pre * (1.0 - sigma))


def per_device(volumes, w_first, w_second, w_third, map_grad):
    full_pads = ((1, 1), (1, 1), (1, 1))
    slab_pads = ((0, 0), (1, 1), (1, 1))
    lower_rim = shifted(volumes[:, :, -1:], "slab", 1)
    first_in = jnp.concatenate([lower_rim, volumes], axis=2)
    pre_first = forward(first_in, w_first, 2, slab_pads)
    act_first = jax.nn.silu(pre_first).astype(jnp.bfloat16)
    lower_maps = shifted(act_first[:, :, -1:], "slab", 1)
    second_in = jnp.concatenate([lower_maps, act_first], axis=2)
    pre_second = forward(second_in, w_second, 2, slab_pads)
    act_second = jax.nn.silu(pre_second).astype(jnp.bfloat16)
    sample_maps = lax.all_to_all(act_second, "slab", split_axis=0, concat_axis=2, tiled=True)
    pre_third = forward(sample_maps, w_third, 1, full_pads)
    delta_third = (map_grad.astype(jnp.float32) * silu_slope(pre_third)).astype(jnp.bfloat16)
    grad_third = weight_grad(sample_maps, delta_third, 1, full_pads)
    back_second = interior(spread_back(delta_third, w_third, 1), sample_maps.shape).astype(
        jnp.bfloat16
    )
    back_second = lax.all_to_all(back_second, "slab", split_axis=2, concat_axis=0, tiled=True)
    delta_second = (back_second.astype(jnp.float32) * silu_slope(pre_second)).astype(jnp.bfloat16)
    grad_second = weight_grad(second_in, delta_second, 2, slab_pads)
    upper_rim = shifted(delta_second[:, :, :1], "slab", -1)
    extended = jnp.concatenate([delta_second, upper_rim], axis=2)
    back_first = interior(spread_back(extended, w_second, 2), act_first.shape)
    delta_first = (back_first * silu_slope(pre_first)).astype(jnp.bfloat16)
    grad_first = weight_grad(first_in, delta_first, 2, slab_pads)
    grad_first, grad_second, grad_third = lax.psum(
        (grad_first, grad_second, grad_third), ("vol", "slab")
    )
    factor = 1.0 / (map_grad.shape[0] * lax.axis_size("vol") * lax.axis_size("slab"))
    return (grad_first * factor, grad_second * factor, grad_third * factor)


def solution(mesh):
    return jax.shard_map(
        per_device,
        mesh=mesh,
        in_specs=(
            P("vol", None, "slab", None, None),
            P(),
            P(),
            P(),
            P(("vol", "slab"), None, None, None, None),
        ),
        out_specs=(P(), P(), P()),
        check_vma=False,
    )
```

profile of v0, /device:TPU:0, one launch (start us, length us, event | category | flops | bytes accessed | tf_op | source)
XLA Modules:
  0.0 215.7 jit_solution(3907313156765782653)
XLA Ops:
  7.2 0.8 slice.15
  8.0 4.9 %collective-permute-start = (bf16[2,4,1,16,64]{4,3,2,1,0:T(8,128)(2,1)S(1)}, bf16[2,4,1,16,64]{4,3,2,1,0:T(8,128)(2,1)S(1)}, u32[]{:S(2)}, u32[]{:S(2)}) collective-permute-start(bf16[2,4,1,16,64]{4,3,2,1,0:T(8,128)(2,1)S(1)} %slice.15), channel_id=1, source_target_pairs={{0,1},{2,3},{4,5},{6,7},{8,9},{10,11},{12,13},{14,15},{16,17},{18,... | collective-permute-start | bytes 49160 | tf_op jit(solution)/shard_map/ppermute | solution.py:14
  12.9 0.8 copy.132
  13.7 0.7 collective-permute-done
  14.5 1.0 constant_dynamic-update-slice_fusion
  15.5 0.2 pad.clone
  15.6 1.5 reshape.38
  17.2 0.7 slice.34
  17.9 3.0 %fusion.2 = bf16[4,9,16,2,8,12]{5,4,2,3,1,0:T(8,128)(2,1)} fusion(bf16[4,9,16,2,7,2]{5,4,2,3,1,0:T(8,128)(2,1)S(1)} %slice.34, bf16[4,9,16,2,8,10]{5,4,2,3,1,0:T(8,128)(2,1)S(1)} %reshape.38), kind=kLoop, calls=%fused_computation.4 | loop fusion | flops 663552 | bytes 437760 | tf_op jit(solution)/shard_map/conv_general_dilated | solution.py:27
  20.9 5.2 %copy.131 = bf16[4,9,16,2,8,12]{2,4,3,5,1,0:T(8,128)(2,1)S(1)} copy(bf16[4,9,16,2,8,12]{5,4,2,3,1,0:T(8,128)(2,1)} %fusion.2) | data formatting | bytes 442368 | tf_op jit(solution)/shard_map/conv_general_dilated | solution.py:27
  26.1 2.4 %copy.133 = bf16[4,9,16,16,12]{3,0,4,2,1:T(4,128)(2,1)} copy(bf16[4,9,16,16,12]{2,3,4,1,0:T(8,128)(2,1)S(1)} %bitcast.102) | data formatting | bytes 442368 | tf_op jit(solution)/shard_map/conv_general_dilated | solution.py:27
  28.5 4.7 %multiply_convert_fusion = (bf16[4,8,16,5,32]{4,2,3,1,0:T(8,128)(2,1)S(1)}, f32[4,8,16,5,32]{4,2,3,1,0:T(8,128)}) fusion(bf16[4,9,16,16,12]{3,0,4,2,1:T(4,128)(2,1)} %copy.133, bf16[32,3,3,3,4]{0,4,3,2,1:T(4,128)(2,1)S(1)} %reshape.30, pred[16,5]{0,1:T(8,128)(4,1)S(1)} %copy-done.5), kind=kOutput, calls=%fused_computation.14 | convolution fusion | flops 17776640 | bytes 719696 | tf_op jit(solution)/shard_map/conv_general_dilated | solution.py:27
  33.4 0.1 copy.194
  33.5 4.2 %collective-permute-start.1 = (bf16[2,32,1,8,32]{1,0,4,3,2:T(2,128)(2,1)S(1)}, bf16[2,32,1,8,32]{1,0,4,3,2:T(2,128)(2,1)S(1)}, u32[]{:S(2)}, u32[]{:S(2)}) collective-permute-start(bf16[2,32,1,8,32]{1,0,4,3,2:T(2,128)(2,1)S(1)} %bitcast.129), channel_id=1, source_target_pairs={{0,1},{2,3},{4,5},{6,7},{8,9},{10,11},{12,13},{14,15},{16,17},{18,... | collective-permute-start | bytes 98312 | tf_op jit(solution)/shard_map/ppermute | solution.py:14
  37.7 0.2 copy.140
  37.9 0.2 copy.136
  38.1 0.5 copy.193
  38.7 1.5 collective-permute-done.1
  40.2 1.0 fusion.55
  41.2 0.9 pad.2
  42.1 0.2 copy.139
  42.5 0.3 copy-done.7
  42.8 0.8 multiply_convert_fusion.1
  43.7 0.7 reshape.100
  44.5 3.7 %all-to-all-start = ((bf16[2,2,4096]{2,1,0:T(2,128)(2,1)}), bf16[2,2,4096]{2,1,0:T(2,128)(2,1)S(1)}, u32[]{:S(2)}, u32[]{:S(2)}) async-start(bf16[2,2,4096]{2,1,0:T(2,128)(2,1)} %reshape.100), calls=%async_computation | async-start | bytes 65536 | tf_op jit(solution)/shard_map/all_to_all | solution.py:89
  48.2 8.7 %copy.159 = bf16[2,4,9,16,64]{1,0,4,3,2:T(2,128)(2,1)} copy(bf16[2,4,9,16,64]{4,3,2,1,0:T(8,128)(2,1)S(1)} %constant_dynamic-update-slice_fusion) | data formatting | bytes 294912 | tf_op jit(solution)/shard_map/concatenate | solution.py:82
  56.8 1.7 copy.158
  58.7 0.1 reshape.101
  59.0 0.6 add_multiply_fusion.1
  59.8 0.8 fusion.10
  60.7 0.7 reshape.102
  61.5 3.5 %all-to-all-start.1 = ((bf16[2,2,4096]{2,1,0:T(2,128)(2,1)}), bf16[2,2,4096]{2,1,0:T(2,128)(2,1)S(1)}, u32[]{:S(2)}, u32[]{:S(2)}) async-start(bf16[2,2,4096]{2,1,0:T(2,128)(2,1)} %reshape.102), calls=%async_computation.1 | async-start | bytes 65536 | tf_op jit(solution)/shard_map/all_to_all | solution.py:96
  64.9 2.5 %fusion.39 = f32[128,3,3,3,64]{0,4,3,2,1:T(8,128)} fusion(bf16[1,128,4,4,16]{1,3,4,2,0:T(4,128)(2,1)S(1)} %fusion.36, bf16[1,64,4,4,16]{1,4,3,2,0:T(8,128)(2,1)S(1)} %bitcast.112), kind=kOutput, calls=%fused_computation.57 | convolution fusion | flops 75366400 | bytes 983040 | tf_op jit(solution)/shard_map/transpose | solution.py:23
  67.5 1.4 all-to-all-done.1
  69.1 1.3 collective-permute-start.2
  70.4 1.6 fusion.44
  72.0 0.9 copy.162
  72.8 2.0 collective-permute-done.2
  75.0 0.1 pad.8.clone
  75.2 0.2 fusion.20
  75.4 0.8 convolution_select_fusion
  76.3 0.9 copy.157
  77.3 11.5 %fusion.16 = f32[32,3,3,3,4]{0,4,3,2,1:T(4,128)S(1)} fusion(bf16[2,4,9,16,64]{1,0,4,3,2:T(2,128)(2,1)} %copy.159, bf16[4,8,2,32,32]{4,1,3,2,0:T(8,128)(2,1)S(1)} %fusion.14), kind=kOutput, calls=%fused_computation.26 | convolution fusion | flops 13424640 | bytes 292352 | tf_op jit(solution)/shard_map/transpose | solution.py:23
  88.9 40.4 %psum.21 = f32[32,108]{0,1:T(8,128)S(1)} all-reduce(f32[32,108]{0,1:T(8,128)S(1)} %reshape.33), channel_id=1, replica_groups=mesh['vol'=16,'slab'=2] {'vol','slab'}, use_global_device_ids=true, to_apply=%region_0.1 | all-reduce | flops 3456 | bytes 27648 | tf_op jit(solution)/shard_map/psum | solution.py:104
  129.2 0.7 copy.165
  129.9 76.0 %all-reduce.3.cloned.1.call-done = (f32[64,864]{1,0:T(8,128)}, f32[128,1728]{0,1:T(8,128)}) async-done(((f32[64,864]{1,0:T(8,128)}, f32[128,1728]{0,1:T(8,128)}), (f32[64,864]{1,0:T(8,128)}, f32[128,1728]{0,1:T(8,128)})) %all-reduce.3.cloned.1.call-update) | async-done | bytes 1105936 | tf_op jit(solution)/shard_map/psum | solution.py:104
  206.0 2.2 %broadcast_multiply_fusion = f32[128,1728]{0,1:T(8,128)} fusion(f32[128,1728]{0,1:T(8,128)} %get-tuple-element.16), kind=kLoop, calls=%fused_computation.28 | loop fusion | flops 221184 | bytes 1769472 | tf_op jit(solution)/shard_map/mul | solution.py:108
  208.1 0.7 broadcast_multiply_fusion.1
  (52 shorter events, 1.2 us)
Async XLA Ops:
  7.2 51.8 %copy-start = (bf16[128,1728]{0,1:T(8,128)(2,1)S(1)}, bf16[128,1728]{0,1:T(8,128)(2,1)}, u32[]{:S(2)}) copy-start(bf16[128,1728]{0,1:T(8,128)(2,1)} %param.8) | copy-start | bytes 1327108
  8.0 6.4 %collective-permute-start = (bf16[2,4,1,16,64]{4,3,2,1,0:T(8,128)(2,1)S(1)}, bf16[2,4,1,16,64]{4,3,2,1,0:T(8,128)(2,1)S(1)}, u32[]{:S(2)}, u32[]{:S(2)}) collective-permute-start(bf16[2,4,1,16,64]{4,3,2,1,0:T(8,128)(2,1)S(1)} %slice.15), channel_id=1, source_target_pairs={{0,1},{2,3},{4,5},{6,7},{8,9},{10,11},{12,13},{14,15},{16,17},{18,... | collective-permute-start | bytes 49160 | tf_op jit(solution)/shard_map/ppermute | solution.py:14
  26.1 2.4 %copy-start.5 = (pred[16,5]{0,1:T(8,128)(4,1)S(1)}, pred[16,5]{0,1:T(8,128)(4,1)}, u32[]{:S(2)}) copy-start(pred[16,5]{0,1:T(8,128)(4,1)} %constant.38) | copy-start | bytes 244
  28.5 9.2 %copy-start.2 = (bf16[64,864]{1,0:T(8,128)(2,1)S(1)}, bf16[64,864]{1,0:T(8,128)(2,1)}, u32[]{:S(2)}) copy-start(bf16[64,864]{1,0:T(8,128)(2,1)} %param.7) | copy-start | bytes 331780
  33.5 6.7 %collective-permute-start.1 = (bf16[2,32,1,8,32]{1,0,4,3,2:T(2,128)(2,1)S(1)}, bf16[2,32,1,8,32]{1,0,4,3,2:T(2,128)(2,1)S(1)}, u32[]{:S(2)}, u32[]{:S(2)}) collective-permute-start(bf16[2,32,1,8,32]{1,0,4,3,2:T(2,128)(2,1)S(1)} %bitcast.129), channel_id=1, source_target_pairs={{0,1},{2,3},{4,5},{6,7},{8,9},{10,11},{12,13},{14,15},{16,17},{18,... | collective-permute-start | bytes 98312 | tf_op jit(solution)/shard_map/ppermute | solution.py:14
  42.1 0.7 copy-start.7
  44.5 14.2 %all-to-all-start = ((bf16[2,2,4096]{2,1,0:T(2,128)(2,1)}), bf16[2,2,4096]{2,1,0:T(2,128)(2,1)S(1)}, u32[]{:S(2)}, u32[]{:S(2)}) async-start(bf16[2,2,4096]{2,1,0:T(2,128)(2,1)} %reshape.100), calls=%async_computation | async-start | bytes 65536 | tf_op jit(solution)/shard_map/all_to_all | solution.py:89
  56.8 2.1 copy-start.6
  58.7 1.0 copy-start.3
  61.5 7.4 %all-to-all-start.1 = ((bf16[2,2,4096]{2,1,0:T(2,128)(2,1)}), bf16[2,2,4096]{2,1,0:T(2,128)(2,1)S(1)}, u32[]{:S(2)}, u32[]{:S(2)}) async-start(bf16[2,2,4096]{2,1,0:T(2,128)(2,1)} %reshape.102), calls=%async_computation.1 | async-start | bytes 65536 | tf_op jit(solution)/shard_map/all_to_all | solution.py:96
  64.9 141.0 %all-reduce.3.cloned.1.call-start = ((), (), s32[]{:S(2)}) async-start(), calls=%async_computation.2 | async-start | bytes 2228224 | tf_op jit(solution)/shard_map/psum | solution.py:104
  69.1 5.8 %collective-permute-start.2 = (bf16[2,64,1,4,16]{1,4,3,2,0:T(8,128)(2,1)S(1)}, bf16[2,64,1,4,16]{1,4,3,2,0:T(8,128)(2,1)S(1)}, u32[]{:S(2)}, u32[]{:S(2)}) collective-permute-start(bf16[2,64,1,4,16]{1,4,3,2,0:T(8,128)(2,1)S(1)} %slice.45), channel_id=1, source_target_pairs={{1,0},{3,2},{5,4},{7,6},{9,8},{11,10},{13,12},{15,14},{17,16},{19,... | collective-permute-start | bytes 49160 | tf_op jit(solution)/shard_map/ppermute | solution.py:14
  71.9 3.5 %copy-start.4 = (pred[16,6]{0,1:T(8,128)(4,1)S(1)}, pred[16,6]{0,1:T(8,128)(4,1)}, u32[]{:S(2)}) copy-start(pred[16,6]{0,1:T(8,128)(4,1)} %constant.34) | copy-start | bytes 292
  206.0 2.2 %copy-start.1 = (f32[64,864]{1,0:T(8,128)S(1)}, f32[64,864]{1,0:T(8,128)}, u32[]{:S(2)}) copy-start(f32[64,864]{1,0:T(8,128)} %get-tuple-element.15) | copy-start | bytes 663556
Sparse Core Ops, SparseCore 0:
  73.0 132.9 all-reduce.2
where the time goes:
time: 216 us
  waiting for transfers between devices  81.7 us (38%)
  blocking collectives  40.4 us (19%)
  local copies, waits for them, and re-layouts  30.6 us (14%)
  matrix products  23.5 us (11%)
  starting transfers between devices  17.6 us (8%)
  between operations  14.5 us (7%)
  other arithmetic  7.37 us (3%)
    psum x1, waiting for transfers between devices, per_device(): lax.psum((grad_first, grad_second, grad_third), ('vol', 'slab'))  76 us
    psum x1, blocking collectives, per_device(): lax.psum((grad_first, grad_second, grad_third), ('vol', 'slab'))  40.4 us
    transpose x3, matrix products, flat_of(): return kernel.transpose(0, 2, 3, 4, 1).reshape(kernel.shape[0], -1)  15.6 us
    ppermute x3, starting transfers between devices, shifted(): return lax.ppermute(array, axis, pairs)  10.4 us
    conv_general_dilated x8, local copies, waits for them, and re-layouts, forward(): lax.conv_general_dilated(maps, kernel_of(weight), (stride, stride, stride...  10.1 us
    concatenate x3, local copies, waits for them, and re-layouts, per_device(): first_in = jnp.concatenate([lower_rim, volumes], axis=2)  9.8 us
    conv_general_dilated x3, matrix products, forward(): lax.conv_general_dilated(maps, kernel_of(weight), (stride, stride, stride...  6.18 us
    unnamed x31, local copies, waits for them, and re-layouts  4.63 us
  transfers between devices with their start and end apart: 6, of which 5 were waited for; matrix products, arithmetic and copies ran while one was open for 15% of the time, Pallas kernels for 0%

commit v1 on v0

--- a/solution.py
+++ b/solution.py
@@ -1,11 +1,28 @@
+import functools
 import jax
 import jax.numpy as jnp
 from jax import lax
 from jax.sharding import PartitionSpec as P
+from jax.lax import all_to_all, axis_size
 
 FORWARD_DIMS = ("NCDHW", "OIDHW", "NCDHW")
 FILTER_DIMS = ("CNDHW", "IODHW", "CNDHW")
 SPREAD_DIMS = ("NCDHW", "IODHW", "NCDHW")
+
+
+def serve_cube_up(my_data, row_axis):
+    return jnp.concatenate(
+        all_to_all(
+            jnp.stack(jnp.split(my_data, axis_size(row_axis), 2)),
+            axis_name=row_axis,
+            split_axis=0,
+            concat_axis=0,
+        ),
+        0,
+    )
+
+
+lift_targets_on_mesh = functools.partial(serve_cube_up, row_axis="slab")
 
 
 def shifted(array, axis, by):
@@ -93,7 +110,7 @@
     back_second = interior(spread_back(delta_third, w_third, 1), sample_maps.shape).astype(
         jnp.bfloat16
     )
-    back_second = lax.all_to_all(back_second, "slab", split_axis=2, concat_axis=0, tiled=True)
+    back_second = lift_targets_on_mesh(back_second)
     delta_second = (back_second.astype(jnp.float32) * silu_slope(pre_second)).astype(jnp.bfloat16)
     grad_second = weight_grad(second_in, delta_second, 2, slab_pads)
     upper_rim = shifted(delta_second[:, :, :1], "slab", -1)

time: 216 us -> 216 us (level)
    unnamed x31 -> x30, local copies, waits for them, and re-layouts: 4.63 us -> 4.6 us
where the time goes in v1:
time: 216 us
  waiting for transfers between devices  81.7 us (38%)
  blocking collectives  40.3 us (19%)
  local copies, waits for them, and re-layouts  30.6 us (14%)
  matrix products  23.5 us (11%)
  starting transfers between devices  17.6 us (8%)
  between operations  14.6 us (7%)
  other arithmetic  7.38 us (3%)
    psum x1, waiting for transfers between devices, per_device(): lax.psum((grad_first, grad_second, grad_third), ('vol', 'slab'))  76 us
    psum x1, blocking collectives, per_device(): lax.psum((grad_first, grad_second, grad_third), ('vol', 'slab'))  40.3 us
    transpose x3, matrix products, flat_of(): return kernel.transpose(0, 2, 3, 4, 1).reshape(kernel.shape[0], -1)  15.6 us
    ppermute x3, starting transfers between devices, shifted(): return lax.ppermute(array, axis, pairs)  10.4 us
    conv_general_dilated x8, local copies, waits for them, and re-layouts, forward(): lax.conv_general_dilated(maps, kernel_of(weight), (stride, stride, stride...  10.1 us
    concatenate x3, local copies, waits for them, and re-layouts, per_device(): first_in = jnp.concatenate([lower_rim, volumes], axis=2)  9.76 us
    conv_general_dilated x3, matrix products, forward(): lax.conv_general_dilated(maps, kernel_of(weight), (stride, stride, stride...  6.17 us
    unnamed x30, local copies, waits for them, and re-layouts  4.6 us
  transfers between devices with their start and end apart: 6, of which 5 were waited for; matrix products, arithmetic and copies ran while one was open for 15% of the time, Pallas kernels for 0%

profile of v1, /device:TPU:0, one launch (start us, length us, event | category | flops | bytes accessed | tf_op | source)
XLA Modules:
  0.0 215.6 jit_solution(8688615663429315844)
XLA Ops:
  7.2 0.8 slice.15
  8.0 4.9 %collective-permute-start = (bf16[2,4,1,16,64]{4,3,2,1,0:T(8,128)(2,1)S(1)}, bf16[2,4,1,16,64]{4,3,2,1,0:T(8,128)(2,1)S(1)}, u32[]{:S(2)}, u32[]{:S(2)}) collective-permute-start(bf16[2,4,1,16,64]{4,3,2,1,0:T(8,128)(2,1)S(1)} %slice.15), channel_id=1, source_target_pairs={{0,1},{2,3},{4,5},{6,7},{8,9},{10,11},{12,13},{14,15},{16,17},{18,... | collective-permute-start | bytes 49160 | tf_op jit(solution)/shard_map/ppermute | solution.py:31
  12.9 0.8 copy.137
  13.7 0.7 collective-permute-done
  14.5 1.0 constant_dynamic-update-slice_fusion
  15.5 0.2 pad.clone
  15.6 1.5 reshape.37
  17.2 0.7 slice.37
  17.9 3.0 %fusion.2 = bf16[4,9,16,2,8,12]{5,4,2,3,1,0:T(8,128)(2,1)} fusion(bf16[4,9,16,2,7,2]{5,4,2,3,1,0:T(8,128)(2,1)S(1)} %slice.37, bf16[4,9,16,2,8,10]{5,4,2,3,1,0:T(8,128)(2,1)S(1)} %reshape.37), kind=kLoop, calls=%fused_computation.4 | loop fusion | flops 663552 | bytes 437760 | tf_op jit(solution)/shard_map/conv_general_dilated | solution.py:44
  20.9 5.2 %copy.136 = bf16[4,9,16,2,8,12]{2,4,3,5,1,0:T(8,128)(2,1)S(1)} copy(bf16[4,9,16,2,8,12]{5,4,2,3,1,0:T(8,128)(2,1)} %fusion.2) | data formatting | bytes 442368 | tf_op jit(solution)/shard_map/conv_general_dilated | solution.py:44
  26.1 2.4 %copy.138 = bf16[4,9,16,16,12]{3,0,4,2,1:T(4,128)(2,1)} copy(bf16[4,9,16,16,12]{2,3,4,1,0:T(8,128)(2,1)S(1)} %bitcast.103) | data formatting | bytes 442368 | tf_op jit(solution)/shard_map/conv_general_dilated | solution.py:44
  28.5 4.7 %multiply_convert_fusion = (bf16[4,8,16,5,32]{4,2,3,1,0:T(8,128)(2,1)S(1)}, f32[4,8,16,5,32]{4,2,3,1,0:T(8,128)}) fusion(bf16[4,9,16,16,12]{3,0,4,2,1:T(4,128)(2,1)} %copy.138, bf16[32,3,3,3,4]{0,4,3,2,1:T(4,128)(2,1)S(1)} %reshape.29, pred[16,5]{0,1:T(8,128)(4,1)S(1)} %copy-done.5), kind=kOutput, calls=%fused_computation.14 | convolution fusion | flops 17776640 | bytes 719696 | tf_op jit(solution)/shard_map/conv_general_dilated | solution.py:44
  33.3 0.1 copy.202
  33.4 4.2 %collective-permute-start.1 = (bf16[2,32,1,8,32]{1,0,4,3,2:T(2,128)(2,1)S(1)}, bf16[2,32,1,8,32]{1,0,4,3,2:T(2,128)(2,1)S(1)}, u32[]{:S(2)}, u32[]{:S(2)}) collective-permute-start(bf16[2,32,1,8,32]{1,0,4,3,2:T(2,128)(2,1)S(1)} %bitcast.129), channel_id=1, source_target_pairs={{0,1},{2,3},{4,5},{6,7},{8,9},{10,11},{12,13},{14,15},{16,17},{18,... | collective-permute-start | bytes 98312 | tf_op jit(solution)/shard_map/ppermute | solution.py:31
  37.7 0.2 copy.145
  37.9 0.2 copy.141
  38.1 0.5 copy.201
  38.6 1.5 collective-permute-done.1
  40.2 1.0 fusion.55
  41.2 0.9 pad.2
  42.1 0.2 copy.144
  42.4 0.3 copy-done.7
  42.7 0.8 multiply_convert_fusion.1
  43.7 0.7 reshape.101
  44.4 3.7 %all-to-all-start = ((bf16[2,2,4096]{2,1,0:T(2,128)(2,1)}), bf16[2,2,4096]{2,1,0:T(2,128)(2,1)S(1)}, u32[]{:S(2)}, u32[]{:S(2)}) async-start(bf16[2,2,4096]{2,1,0:T(2,128)(2,1)} %reshape.101), calls=%async_computation | async-start | bytes 65536 | tf_op jit(solution)/shard_map/all_to_all | solution.py:106
  48.1 8.6 %copy.165 = bf16[2,4,9,16,64]{1,0,4,3,2:T(2,128)(2,1)} copy(bf16[2,4,9,16,64]{4,3,2,1,0:T(8,128)(2,1)S(1)} %constant_dynamic-update-slice_fusion) | data formatting | bytes 294912 | tf_op jit(solution)/shard_map/concatenate | solution.py:99
  56.8 1.7 copy.164
  58.6 0.1 reshape.102
  58.9 0.6 add_multiply_fusion.1
  59.7 0.8 fusion.10
  60.7 0.7 reshape.103
  61.5 3.5 %all-to-all-start.1 = ((bf16[2,2,4096]{2,1,0:T(2,128)(2,1)}), bf16[2,2,4096]{2,1,0:T(2,128)(2,1)S(1)}, u32[]{:S(2)}, u32[]{:S(2)}) async-start(bf16[2,2,4096]{2,1,0:T(2,128)(2,1)} %reshape.103), calls=%async_computation.1 | async-start | bytes 65536 | tf_op jit(solution)/shard_map/all_to_all | solution.py:15
  64.9 2.5 %fusion.39 = f32[128,3,3,3,64]{0,4,3,2,1:T(8,128)} fusion(bf16[1,128,4,4,16]{1,3,4,2,0:T(4,128)(2,1)S(1)} %fusion.36, bf16[1,64,4,4,16]{1,4,3,2,0:T(8,128)(2,1)S(1)} %bitcast.113), kind=kOutput, calls=%fused_computation.57 | convolution fusion | flops 75366400 | bytes 983040 | tf_op jit(solution)/shard_map/transpose | solution.py:40
  67.5 1.4 all-to-all-done.1
  69.0 1.3 collective-permute-start.2
  70.3 1.6 fusion.44
  71.9 0.9 copy.168
  72.8 2.0 collective-permute-done.2
  75.0 0.1 pad.8.clone
  75.2 0.2 fusion.20
  75.4 0.8 convolution_select_fusion
  76.2 0.9 copy.163
  77.3 11.5 %fusion.16 = f32[32,3,3,3,4]{0,4,3,2,1:T(4,128)S(1)} fusion(bf16[2,4,9,16,64]{1,0,4,3,2:T(2,128)(2,1)} %copy.165, bf16[4,8,2,32,32]{4,1,3,2,0:T(8,128)(2,1)S(1)} %fusion.14), kind=kOutput, calls=%fused_computation.26 | convolution fusion | flops 13424640 | bytes 292352 | tf_op jit(solution)/shard_map/transpose | solution.py:40
  88.8 40.3 %psum.21 = f32[32,108]{0,1:T(8,128)S(1)} all-reduce(f32[32,108]{0,1:T(8,128)S(1)} %reshape.32), channel_id=1, replica_groups=mesh['vol'=16,'slab'=2] {'vol','slab'}, use_global_device_ids=true, to_apply=%region_0.1 | all-reduce | flops 3456 | bytes 27648 | tf_op jit(solution)/shard_map/psum | solution.py:121
  129.2 0.7 copy.171
  129.9 76.0 %all-reduce.3.cloned.1.call-done = (f32[64,864]{1,0:T(8,128)}, f32[128,1728]{0,1:T(8,128)}) async-done(((f32[64,864]{1,0:T(8,128)}, f32[128,1728]{0,1:T(8,128)}), (f32[64,864]{1,0:T(8,128)}, f32[128,1728]{0,1:T(8,128)})) %all-reduce.3.cloned.1.call-update) | async-done | bytes 1105936 | tf_op jit(solution)/shard_map/psum | solution.py:121
  205.9 2.2 %broadcast_multiply_fusion = f32[128,1728]{0,1:T(8,128)} fusion(f32[128,1728]{0,1:T(8,128)} %get-tuple-element.16), kind=kLoop, calls=%fused_computation.28 | loop fusion | flops 221184 | bytes 1769472 | tf_op jit(solution)/shard_map/mul | solution.py:125
  208.1 0.7 broadcast_multiply_fusion.1
  (56 shorter events, 1.3 us)
Async XLA Ops:
  7.2 51.7 %copy-start = (bf16[128,1728]{0,1:T(8,128)(2,1)S(1)}, bf16[128,1728]{0,1:T(8,128)(2,1)}, u32[]{:S(2)}) copy-start(bf16[128,1728]{0,1:T(8,128)(2,1)} %param.8) | copy-start | bytes 1327108
  8.0 6.4 %collective-permute-start = (bf16[2,4,1,16,64]{4,3,2,1,0:T(8,128)(2,1)S(1)}, bf16[2,4,1,16,64]{4,3,2,1,0:T(8,128)(2,1)S(1)}, u32[]{:S(2)}, u32[]{:S(2)}) collective-permute-start(bf16[2,4,1,16,64]{4,3,2,1,0:T(8,128)(2,1)S(1)} %slice.15), channel_id=1, source_target_pairs={{0,1},{2,3},{4,5},{6,7},{8,9},{10,11},{12,13},{14,15},{16,17},{18,... | collective-permute-start | bytes 49160 | tf_op jit(solution)/shard_map/ppermute | solution.py:31
  26.1 2.4 %copy-start.5 = (pred[16,5]{0,1:T(8,128)(4,1)S(1)}, pred[16,5]{0,1:T(8,128)(4,1)}, u32[]{:S(2)}) copy-start(pred[16,5]{0,1:T(8,128)(4,1)} %constant.38) | copy-start | bytes 244
  28.5 9.2 %copy-start.2 = (bf16[64,864]{1,0:T(8,128)(2,1)S(1)}, bf16[64,864]{1,0:T(8,128)(2,1)}, u32[]{:S(2)}) copy-start(bf16[64,864]{1,0:T(8,128)(2,1)} %param.7) | copy-start | bytes 331780
  33.4 6.7 %collective-permute-start.1 = (bf16[2,32,1,8,32]{1,0,4,3,2:T(2,128)(2,1)S(1)}, bf16[2,32,1,8,32]{1,0,4,3,2:T(2,128)(2,1)S(1)}, u32[]{:S(2)}, u32[]{:S(2)}) collective-permute-start(bf16[2,32,1,8,32]{1,0,4,3,2:T(2,128)(2,1)S(1)} %bitcast.129), channel_id=1, source_target_pairs={{0,1},{2,3},{4,5},{6,7},{8,9},{10,11},{12,13},{14,15},{16,17},{18,... | collective-permute-start | bytes 98312 | tf_op jit(solution)/shard_map/ppermute | solution.py:31
  42.1 0.7 copy-start.7
  44.4 14.2 %all-to-all-start = ((bf16[2,2,4096]{2,1,0:T(2,128)(2,1)}), bf16[2,2,4096]{2,1,0:T(2,128)(2,1)S(1)}, u32[]{:S(2)}, u32[]{:S(2)}) async-start(bf16[2,2,4096]{2,1,0:T(2,128)(2,1)} %reshape.101), calls=%async_computation | async-start | bytes 65536 | tf_op jit(solution)/shard_map/all_to_all | solution.py:106
  56.8 2.1 copy-start.6
  58.6 1.0 copy-start.3
  61.5 7.4 %all-to-all-start.1 = ((bf16[2,2,4096]{2,1,0:T(2,128)(2,1)}), bf16[2,2,4096]{2,1,0:T(2,128)(2,1)S(1)}, u32[]{:S(2)}, u32[]{:S(2)}) async-start(bf16[2,2,4096]{2,1,0:T(2,128)(2,1)} %reshape.103), calls=%async_computation.1 | async-start | bytes 65536 | tf_op jit(solution)/shard_map/all_to_all | solution.py:15
  64.9 141.0 %all-reduce.3.cloned.1.call-start = ((), (), s32[]{:S(2)}) async-start(), calls=%async_computation.2 | async-start | bytes 2228224 | tf_op jit(solution)/shard_map/psum | solution.py:121
  69.0 5.8 %collective-permute-start.2 = (bf16[2,64,1,4,16]{1,4,3,2,0:T(8,128)(2,1)S(1)}, bf16[2,64,1,4,16]{1,4,3,2,0:T(8,128)(2,1)S(1)}, u32[]{:S(2)}, u32[]{:S(2)}) collective-permute-start(bf16[2,64,1,4,16]{1,4,3,2,0:T(8,128)(2,1)S(1)} %slice.51), channel_id=1, source_target_pairs={{1,0},{3,2},{5,4},{7,6},{9,8},{11,10},{13,12},{15,14},{17,16},{19,... | collective-permute-start | bytes 49160 | tf_op jit(solution)/shard_map/ppermute | solution.py:31
  71.9 3.5 %copy-start.4 = (pred[16,6]{0,1:T(8,128)(4,1)S(1)}, pred[16,6]{0,1:T(8,128)(4,1)}, u32[]{:S(2)}) copy-start(pred[16,6]{0,1:T(8,128)(4,1)} %constant.34) | copy-start | bytes 292
  205.9 2.2 %copy-start.1 = (f32[64,864]{1,0:T(8,128)S(1)}, f32[64,864]{1,0:T(8,128)}, u32[]{:S(2)}) copy-start(f32[64,864]{1,0:T(8,128)} %get-tuple-element.15) | copy-start | bytes 663556
Sparse Core Ops, SparseCore 0:
  72.9 132.9 all-reduce.2
